TPU v7x, 512 devices: a whole 4x8x8 slice. The times are simulated.
512 devices in a mesh: tm: 64 (over y, z_lo, core), sta: 8 (over x, z_hi).
Axes of the slice: x: 4, y: 8, z: 8 (z_hi: 2, z_lo: 4; z = z_hi * 4 + z_lo), core: 2. Of those that a mesh axis runs over, the one named last changes fastest.
Arguments:
- data: bfloat16 [64, 3, 24576], P('sta', None, 'tm'), as said below
- bank: bfloat16 [64, 8, 64, 3, 150], P('tm', None, 'sta'), may hold values from -6 to 6
- owners: int32 [2], replicated, may hold values from 0 to 63
- moveouts: int32 [2, 8, 64], P(None, None, 'sta'), may hold values from 0 to 64, as said below
Outputs:
- stack: float32 [2, 8, 24576], P(None, 'sta', 'tm')
Inputs may be any that keep to these rules, and one draw needn't show every extreme that they name: `data`: three-component records with amplitudes that vary from station to station and along time. `moveouts`: delays are relative to the earliest arrival: for each template some station has 0 and some other station has 64.
All inputs are finite; a program needn't handle non-finite values.
Results may differ from a plain program's by a relative error of at most 0.0003.
Values may be sent and summed in bfloat16 or wider, within the bound.
No kernel may reach another device: no remote copies, remote signals or barrier semaphores. Data moves between devices by JAX's collectives and lax.ppermute only.
A program may use at most 64 MiB of HBM per device.

v0:
```python
import jax
import jax.numpy as jnp
from jax import lax
from jax.sharding import PartitionSpec as P

MAXM = 64
eps = 1e-06


def passed_along(block, axis, distance):
    devices = range(lax.axis_size(axis))
    route = [(i - distance, i) for i in devices if i - distance in devices]
    return lax.ppermute(block, axis, route)


def correlate(window, batches):
    batch_count, tmpl_count, local_sta, comp_count, span_len = batches.shape
    kernels = jnp.transpose(batches, (2, 0, 1, 3, 4)).reshape(
        local_sta * batch_count * tmpl_count, comp_count, span_len
    )
    records = window.reshape(1, local_sta * comp_count, window.shape[2])
    products = lax.conv_general_dilated(
        records,
        kernels,
        (1,),
        "VALID",
        dimension_numbers=("NCH", "OIH", "NCH"),
        feature_group_count=local_sta,
        preferred_element_type=jnp.float32,
    )
    products = products.reshape(local_sta, batch_count * tmpl_count, products.shape[2])
    squares = jnp.sum(jnp.square(window.astype(jnp.float32)), axis=1)
    energy = lax.reduce_window(squares, 0.0, lax.add, (1, span_len), (1, 1), "VALID") / (
        comp_count * span_len
    )
    tmpl_power = jnp.sum(jnp.square(batches.astype(jnp.float32)), axis=(3, 4)) / (
        comp_count * span_len
    )
    tmpl_power = jnp.transpose(tmpl_power, (2, 0, 1)).reshape(local_sta, batch_count * tmpl_count)
    return products / (
        comp_count
        * span_len
        * jnp.sqrt(tmpl_power + eps)[:, :, None]
        * jnp.sqrt(energy + eps)[None, :, :].transpose(1, 0, 2)
    )


def shift_rows(scores, lag_table, stretch_len):

    def one_row(row, lag_value):
        return lax.dynamic_slice_in_dim(row, lag_value, stretch_len, 0)

    return jax.vmap(jax.vmap(one_row))(scores, lag_table)


def shards(data, bank, owners, moveouts):
    local_sta, comp_count, stretch_len = data.shape
    span_len = bank.shape[-1]
    tmpl_count = bank.shape[1]
    batch_count = owners.shape[0]
    owned_bank = bank[0]
    device_pos = lax.axis_index("tm")
    masked = jnp.stack(
        [
            jnp.where(owners[batch_id] == device_pos, owned_bank.astype(jnp.float32), 0.0)
            for batch_id in range(batch_count)
        ]
    )
    batches = lax.psum(masked, "tm").astype(jnp.bfloat16)
    edge_cells = passed_along(data[:, :, : span_len - 1 + MAXM], "tm", -1)
    scores = correlate(jnp.concatenate([data, edge_cells], axis=2), batches)
    lag_table = jnp.transpose(moveouts, (2, 0, 1)).reshape(local_sta, batch_count * tmpl_count)
    shifted = shift_rows(scores, lag_table, stretch_len)
    partial_sum = jnp.sum(shifted, axis=0).reshape(batch_count, tmpl_count, stretch_len)
    return lax.psum_scatter(partial_sum, "sta", scatter_dimension=1, tiled=True)


def solution(mesh):
    placed = (P("sta", None, "tm"), P("tm", None, "sta", None, None), P(), P(None, None, "sta"))
    return jax.shard_map(
        shards, mesh=mesh, in_specs=placed, out_specs=P(None, "sta", "tm"), check_vma=False
    )
```

profile of v0, /device:TPU:2, one launch (start us, length us, event | category | flops | bytes accessed | tf_op | source)
XLA Modules:
  0.0 800.6 jit_solution(17727927830055742186)
XLA Ops:
  6.4 277.5 %all-reduce.2 = bf16[2,8,8,3,150]{4,1,0,3,2:T(8,128)(2,1)S(1)} all-reduce(f32[2,8,8,3,150]{4,1,0,3,2:T(8,128)S(1)} %pad_maximum_fusion), channel_id=1, replica_groups=mesh['tm'=64,'sta'=8] {'tm'}, use_global_device_ids=true, to_apply=%region_0.1 | all-reduce | flops 57600 | bytes 345600 | tf_op jit(solution)/shard_map/psum | solution.py:69
  284.3 2.0 copy.43
  288.9 2.5 copy.42
  291.4 9.1 %reduce_window_sum.9 = f32[8,448]{1,0:T(8,128)S(1)} reduce-window(f32[8,597]{1,0:T(8,128)S(1)} %multiply_reduce_fusion.1, f32[]{:T(128)} %constant.6.clone.1), window={size=1x150}, to_apply=%region_3.4 | reduce-window | flops 534016 | bytes 33444 | tf_op jit(solution)/shard_map/reduce_window_sum | solution.py:33
  301.4 98.9 %fusion.2 = f32[1,8,16,448]{2,0,1,3:T(1,128)S(1)} fusion(bf16[1,8,3,597]{2,0,1,3:T(2,128)(2,1)S(1)} %copy.42, bf16[8,16,3,150]{1,2,0,3:T(4,128)(2,1)} %copy.43), kind=kOutput, calls=%fused_computation.18 | convolution fusion | flops 51609600 | bytes 373232 | tf_op jit(solution)/shard_map/conv_general_dilated | solution.py:22
  401.8 344.8 %while.1 = (s32[]{:T(128)}, f32[8,16,448]{2,1,0:T(8,128)S(1)}, s32[128,3]{0,1:T(4,128)S(1)}, f32[128,384]{1,0:T(8,128)S(1)}, s32[]{:T(128)}, /*index=5*/s32[]{:T(128)}) while((s32[]{:T(128)}, f32[8,16,448]{2,1,0:T(8,128)S(1)}, s32[128,3]{0,1:T(4,128)S(1)}, f32[128,384]{1,0:T(8,128)S(1)}, s32[]{:T(128)}, /*index=5*/s32[]{:T(128)}) %tuple.32), condition=%wide.while_cond, body=%wide.while_body.sunk | while | flops 2 | bytes 6281 | solution.py:51
  402.5 2.0 dynamic-slice_bitcast_fusion.2
  407.9 2.0 dynamic-slice_bitcast_fusion.2
  410.6 2.0 dynamic-slice_bitcast_fusion.2
  416.0 2.0 dynamic-slice_bitcast_fusion.2
  421.3 2.0 dynamic-slice_bitcast_fusion.2
  426.7 2.0 dynamic-slice_bitcast_fusion.2
  432.1 2.0 dynamic-slice_bitcast_fusion.2
  437.5 2.0 dynamic-slice_bitcast_fusion.2
  442.9 2.0 dynamic-slice_bitcast_fusion.2
  448.3 2.0 dynamic-slice_bitcast_fusion.2
  453.7 2.0 dynamic-slice_bitcast_fusion.2
  459.1 2.0 dynamic-slice_bitcast_fusion.2
  461.8 2.0 dynamic-slice_bitcast_fusion.2
  467.1 2.0 dynamic-slice_bitcast_fusion.2
  472.5 2.0 dynamic-slice_bitcast_fusion.2
  477.9 2.0 dynamic-slice_bitcast_fusion.2
  483.3 2.0 dynamic-slice_bitcast_fusion.2
  488.7 2.0 dynamic-slice_bitcast_fusion.2
  494.1 2.0 dynamic-slice_bitcast_fusion.2
  499.5 2.0 dynamic-slice_bitcast_fusion.2
  504.9 2.0 dynamic-slice_bitcast_fusion.2
  510.3 2.0 dynamic-slice_bitcast_fusion.2
  512.9 2.0 dynamic-slice_bitcast_fusion.2
  518.3 2.0 dynamic-slice_bitcast_fusion.2
  523.7 2.0 dynamic-slice_bitcast_fusion.2
  746.7 52.7 %all-reduce = f32[2,8,384]{2,0,1:T(2,128)S(1)} all-reduce(f32[2,8,384]{2,0,1:T(2,128)S(1)} %copy.49), channel_id=2, replica_groups=mesh['tm'=64,'sta'=8] {'sta'}, use_global_device_ids=true, to_apply=%region_5.6.clone | all-reduce | flops 6144 | bytes 49152
  (526 shorter events, 304.2 us)
Async XLA Ops:
  0.0 284.2 %copy-start.4 = (s32[2,8,8]{2,1,0:T(8,128)S(1)}, s32[2,8,8]{2,1,0:T(8,128)}, u32[]{:S(2)}) copy-start(s32[2,8,8]{2,1,0:T(8,128)} %param.7) | copy-start | bytes 1540
  0.7 288.2 %collective-permute-start = (bf16[8,3,213]{2,0,1:T(8,128)(2,1)S(1)}, bf16[8,3,213]{2,0,1:T(8,128)(2,1)S(1)}, u32[]{:S(2)}, u32[]{:S(2)}) collective-permute-start(bf16[8,3,213]{2,0,1:T(8,128)(2,1)S(1)} %slice.9), channel_id=1, source_target_pairs={{8,0},{16,8},{24,16},{32,24},{40,32},{48,40},{56,48},{64,56},{72,6... | collective-permute-start | bytes 30680 | tf_op jit(solution)/shard_map/ppermute | solution.py:13
  301.4 98.9 %copy-start = (f32[8,448]{0,1:T(8,128)S(1)}, f32[8,448]{0,1:T(8,128)}, u32[]{:S(2)}) copy-start(f32[8,448]{0,1:T(8,128)} %copy.46) | copy-start | bytes 43012
  301.4 98.9 %copy-start.3 = (f32[8,16]{1,0:T(8,128)S(1)}, f32[8,16]{1,0:T(8,128)}, u32[]{:S(2)}) copy-start(f32[8,16]{1,0:T(8,128)} %copy.51) | copy-start | bytes 1540
  400.9 0.9 copy-start.1
  400.9 0.9 copy-start.2
where the time goes:
time: 804 us; the launch traced here: 801 us
  local copies, waits for them, and re-layouts  355 us (44%)
  blocking collectives  330 us (41%)
  matrix products  98.9 us (12%)
  other arithmetic  10.8 us (1%)
    gather x512, local copies, waits for them, and re-layouts  342 us
    psum x1, blocking collectives, shards(): batches = lax.psum(masked, 'tm').astype(jnp.bfloat16)  278 us
    conv_general_dilated x1, matrix products, correlate(): lax.conv_general_dilated(records, kernels, (1,), 'VALID', dimension_numbe...  98.9 us
    unnamed x1, blocking collectives  52.7 us
  transfers between devices with their start and end apart: 1, of which 0 were waited for; matrix products, arithmetic and copies ran while one was open for 1% of the time, Pallas kernels for 0%

commit v1 on v0

--- a/solution.py
+++ b/solution.py
@@ -1,3 +1,4 @@
+import functools
 import jax
 import jax.numpy as jnp
 from jax import lax
@@ -5,6 +6,13 @@
 
 MAXM = 64
 eps = 1e-06
+
+
+def remake_weights(piece_in, link_axis):
+    return lax.all_gather(piece_in, link_axis).sum(axis=0)
+
+
+store_widths_in = functools.partial(remake_weights, link_axis="tm")
 
 
 def passed_along(block, axis, distance):
@@ -66,7 +74,7 @@
             for batch_id in range(batch_count)
         ]
     )
-    batches = lax.psum(masked, "tm").astype(jnp.bfloat16)
+    batches = store_widths_in(masked).astype(jnp.bfloat16)
     edge_cells = passed_along(data[:, :, : span_len - 1 + MAXM], "tm", -1)
     scores = correlate(jnp.concatenate([data, edge_cells], axis=2), batches)
     lag_table = jnp.transpose(moveouts, (2, 0, 1)).reshape(local_sta, batch_count * tmpl_count)

time: 804 us -> 691 us (0.86)
  the two profiles are of different devices: /device:TPU:2 before, /device:TPU:8 now
where the time goes in v1:
time: 691 us; the launch traced here: 688 us
  local copies, waits for them, and re-layouts  357 us (52%)
  waiting for transfers between devices  131 us (19%)
  matrix products  98.9 us (14%)
  blocking collectives  54.6 us (8%)
  other arithmetic  21 us (3%)
  between operations  14.9 us (2%)
  starting transfers between devices  7.21 us (1%)
    gather x512, local copies, waits for them, and re-layouts  342 us
    all_gather x1, waiting for transfers between devices, remake_weights(): return lax.all_gather(piece_in, link_axis).sum(axis=0)  131 us
    conv_general_dilated x1, matrix products, correlate(): lax.conv_general_dilated(records, kernels, (1,), 'VALID', dimension_numbe...  98.9 us
    unnamed x1, blocking collectives  54.6 us
  transfers between devices with their start and end apart: 2, of which 1 were waited for; matrix products, arithmetic and copies ran while one was open for 2% of the time, Pallas kernels for 0%

profile of v1, /device:TPU:8, one launch (start us, length us, event | category | flops | bytes accessed | tf_op | source)
XLA Modules:
  0.0 687.5 jit_solution(14592448463182757943)
XLA Ops:
  11.8 7.2 %collective-permute-start = (bf16[8,3,213]{2,0,1:T(8,128)(2,1)S(1)}, bf16[8,3,213]{2,0,1:T(8,128)(2,1)S(1)}, u32[]{:S(2)}, u32[]{:S(2)}) collective-permute-start(bf16[8,3,213]{2,0,1:T(8,128)(2,1)S(1)} %slice.9), channel_id=1, source_target_pairs={{8,0},{16,8},{24,16},{32,24},{40,32},{48,40},{56,48},{64,56},{72,6... | collective-permute-start | bytes 30680 | tf_op jit(solution)/shard_map/ppermute | solution.py:21
  22.4 2.5 copy.31
  24.9 9.1 %reduce_window_sum.9 = f32[8,448]{1,0:T(8,128)S(1)} reduce-window(f32[8,597]{1,0:T(8,128)S(1)} %multiply_reduce_fusion.1, f32[]{:T(128)} %constant.6.clone.1), window={size=1x150}, to_apply=%region_3.4 | reduce-window | flops 534016 | bytes 33444 | tf_op jit(solution)/shard_map/reduce_window_sum | solution.py:41
  34.9 130.9 %all-gather.3.cloned.1.call-done = f32[128,8,8,3,150]{4,2,3,1,0:T(8,128)} async-done(((f32[2,8,8,3,150]{4,2,3,1,0:T(8,128)}), f32[128,8,8,3,150]{4,2,3,1,0:T(8,128)}) %all-gather.3.cloned.1.call-update) | async-done | bytes 14745616 | tf_op jit(solution)/shard_map/all_gather | solution.py:12
  165.8 9.4 %reduce_sum.36 = bf16[2,8,8,3,150]{4,2,3,1,0:T(8,128)(2,1)S(1)} reduce(f32[64,2,8,8,3,150]{5,3,4,2,1,0:T(8,128)} %bitcast.35, f32[]{:T(128)} %constant.6.clone.1), dimensions={0}, to_apply=%region_0.1 | reduce | flops 3628800 | bytes 14860804 | tf_op jit(solution)/shard_map/reduce_sum | solution.py:12
  175.3 3.6 copy.32
  179.6 98.9 %fusion.2 = f32[1,8,16,448]{2,0,1,3:T(1,128)S(1)} fusion(bf16[1,8,3,597]{2,0,1,3:T(2,128)(2,1)S(1)} %copy.31, bf16[8,16,3,150]{1,2,0,3:T(4,128)(2,1)} %copy.32), kind=kOutput, calls=%fused_computation.17 | convolution fusion | flops 51609600 | bytes 373232 | tf_op jit(solution)/shard_map/conv_general_dilated | solution.py:30
  280.0 344.8 %while.1 = (s32[]{:T(128)}, f32[8,16,448]{2,1,0:T(8,128)S(1)}, s32[128,3]{0,1:T(4,128)S(1)}, f32[128,384]{1,0:T(8,128)S(1)}, s32[]{:T(128)}, /*index=5*/s32[]{:T(128)}) while((s32[]{:T(128)}, f32[8,16,448]{2,1,0:T(8,128)S(1)}, s32[128,3]{0,1:T(4,128)S(1)}, f32[128,384]{1,0:T(8,128)S(1)}, s32[]{:T(128)}, /*index=5*/s32[]{:T(128)}) %tuple.33), condition=%wide.while_cond, body=%wide.while_body.sunk | while | flops 2 | bytes 6281 | solution.py:59
  283.4 2.0 dynamic-slice_bitcast_fusion.2
  288.8 2.0 dynamic-slice_bitcast_fusion.2
  294.2 2.0 dynamic-slice_bitcast_fusion.2
  296.9 2.0 dynamic-slice_bitcast_fusion.2
  302.3 2.0 dynamic-slice_bitcast_fusion.2
  307.7 2.0 dynamic-slice_bitcast_fusion.2
  313.0 2.0 dynamic-slice_bitcast_fusion.2
  318.4 2.0 dynamic-slice_bitcast_fusion.2
  323.8 2.0 dynamic-slice_bitcast_fusion.2
  329.2 2.0 dynamic-slice_bitcast_fusion.2
  334.6 2.0 dynamic-slice_bitcast_fusion.2
  340.0 2.0 dynamic-slice_bitcast_fusion.2
  345.4 2.0 dynamic-slice_bitcast_fusion.2
  348.1 2.0 dynamic-slice_bitcast_fusion.2
  353.5 2.0 dynamic-slice_bitcast_fusion.2
  358.8 2.0 dynamic-slice_bitcast_fusion.2
  364.2 2.0 dynamic-slice_bitcast_fusion.2
  369.6 2.0 dynamic-slice_bitcast_fusion.2
  375.0 2.0 dynamic-slice_bitcast_fusion.2
  380.4 2.0 dynamic-slice_bitcast_fusion.2
  385.8 2.0 dynamic-slice_bitcast_fusion.2
  391.2 2.0 dynamic-slice_bitcast_fusion.2
  396.6 2.0 dynamic-slice_bitcast_fusion.2
  624.9 54.6 %all-reduce = f32[2,8,384]{2,0,1:T(2,128)S(1)} all-reduce(f32[2,8,384]{2,0,1:T(2,128)S(1)} %copy.37), channel_id=3, replica_groups=mesh['tm'=64,'sta'=8] {'sta'}, use_global_device_ids=true, to_apply=%region_5.6.clone | all-reduce | flops 6144 | bytes 49152
  (526 shorter events, 308.2 us)
Async XLA Ops:
  6.5 159.2 %all-gather.3.cloned.1.call-start = ((), (), s32[]{:S(2)}) async-start(), calls=%async_computation | async-start | bytes 25559040 | tf_op jit(solution)/shard_map/all_gather | solution.py:12
  11.8 10.7 %collective-permute-start = (bf16[8,3,213]{2,0,1:T(8,128)(2,1)S(1)}, bf16[8,3,213]{2,0,1:T(8,128)(2,1)S(1)}, u32[]{:S(2)}, u32[]{:S(2)}) collective-permute-start(bf16[8,3,213]{2,0,1:T(8,128)(2,1)S(1)} %slice.9), channel_id=1, source_target_pairs={{8,0},{16,8},{24,16},{32,24},{40,32},{48,40},{56,48},{64,56},{72,6... | collective-permute-start | bytes 30680 | tf_op jit(solution)/shard_map/ppermute | solution.py:21
  179.6 98.9 %copy-start = (f32[8,448]{0,1:T(8,128)S(1)}, f32[8,448]{0,1:T(8,128)}, u32[]{:S(2)}) copy-start(f32[8,448]{0,1:T(8,128)} %copy.34) | copy-start | bytes 43012
  179.6 98.9 %copy-start.3 = (f32[8,16]{1,0:T(8,128)S(1)}, f32[8,16]{1,0:T(8,128)}, u32[]{:S(2)}) copy-start(f32[8,16]{1,0:T(8,128)} %copy.41) | copy-start | bytes 1540
  279.1 0.9 copy-start.1
  279.1 0.9 copy-start.2
Sparse Core Ops, SparseCore 0:
  11.2 154.5 all-gather.2
